TPU v7x, 256 devices: a whole 4x4x8 slice. The times are simulated.
256 devices in a mesh: section: 2 (over core), chan: 32 (over z, x), feed: 4 (over y).
Axes of the slice: x: 4, y: 4, z: 8, core: 2. Of those that a mesh axis runs over, the one named last changes fastest.
Arguments:
- voltages: bfloat16 [2, 1024, 24, 8192], P(None, 'feed', 'section', 'chan'), may hold values from -4 to 4
- positions: int32 [1024], replicated, may hold values from 0 to 1023, each once
- chan_delays: int32 [16, 8192], replicated, may hold values from 0 to 2
- sub_delays: int32 [256, 32], replicated, may hold values from 0 to 4
- boxcars: int32 [3, 2], replicated, may hold values from 1 to 6, as said below
Outputs:
- boxcar_snr: float32 [1024, 24, 3, 256], P(('chan', 'feed'), 'section')
Inputs may be any that keep to these rules, and one draw needn't show every extreme that they name: `boxcars`: column 0 holds the widths 2 to 4, each once; column 1 holds dilations of 1 or more with (width - 1) * dilation <= 6; the filter of width 2 has dilation 6 and the widest filter dilation 1.
All inputs are finite; a program needn't handle non-finite values.
Results may differ from a plain program's by a relative error of at most 0.0033.
Values may be sent and summed in bfloat16 or wider, within the bound.
A program may use at most 64 MiB of HBM per device.

v0:
```python
import math

import jax
import jax.numpy as jnp
from jax import lax
from jax.sharding import PartitionSpec as P

NF = 1024
C = 8192
NK = 16
ND = 256
NW = 3
D1MAX = 2
D2MAX = 4
BOXMAX = 6
SUBCH = 256
EPSILON = 1e-05


def beam_order(positions):
    chan = jnp.arange(32, dtype=jnp.int32)[None, :, None]
    feed = jnp.arange(4, dtype=jnp.int32)[:, None, None]
    low = jnp.arange(8, dtype=jnp.int32)[None, None, :]
    beam_ids = (chan * 32 + feed * 8 + low).reshape(NF)
    phase_ids = beam_ids[:, None] * positions[None, :] % NF
    angles = phase_ids.astype(jnp.float32) * (2.0 * math.pi / NF)
    cosine = jnp.cos(angles)
    sine = jnp.sin(angles)
    upper = jnp.concatenate([cosine, sine], axis=1)
    lower = jnp.concatenate([-sine, cosine], axis=1)
    return jnp.concatenate([upper, lower], axis=0).astype(jnp.bfloat16)


def two_part_dot(values, zero_one):
    high = values.astype(jnp.bfloat16)
    low = (values - high.astype(jnp.float32)).astype(jnp.bfloat16)
    first = jnp.dot(high, zero_one, preferred_element_type=jnp.float32)
    return first + jnp.dot(low, zero_one, preferred_element_type=jnp.float32)


def channel_selector(delays, span_t):
    local = delays.shape[1]
    times = jnp.arange(span_t, dtype=jnp.int32)[:, None, None, None]
    outs = jnp.arange(span_t + D1MAX, dtype=jnp.int32)[None, None, :, None]
    chosen = (times + D1MAX - outs) == jnp.transpose(delays)[None, :, None, :]
    return chosen.astype(jnp.bfloat16).reshape(span_t * local, (span_t + D1MAX) * NK)


def subband_selector(sub_delays):
    offsets = jnp.arange(D2MAX + 1, dtype=jnp.int32)[:, None, None, None]
    matches = jnp.transpose(sub_delays)[None, :, None, :] == offsets
    trial_k = jnp.arange(ND, dtype=jnp.int32) * NK // ND
    own = jnp.arange(NK, dtype=jnp.int32)[:, None] == trial_k[None, :]
    weights = matches & own[None, None, :, :]
    return weights.astype(jnp.bfloat16).reshape(D2MAX + 1, -1, ND)


def boxcar_filter(extended, boxcars, span_t):
    outputs = []
    for filter_index in range(NW):
        width_now = boxcars[filter_index, 0]
        stride_now = boxcars[filter_index, 1]
        summed = extended[:, :span_t]
        for offset in range(1, NW + 1):
            start = jnp.minimum(offset * stride_now, BOXMAX)
            window_part = lax.dynamic_slice_in_dim(extended, start, span_t, 1)
            summed = summed + jnp.where(offset < width_now, window_part, 0.0)
        outputs.append(summed * lax.rsqrt(width_now.astype(jnp.float32)))
    return jnp.stack(outputs, axis=2)


def per_device(voltages, positions, chan_delays, sub_delays, boxcars):
    gathered = lax.all_to_all(voltages, "feed", split_axis=3, concat_axis=1, tiled=True)
    span_t = gathered.shape[2]
    local = gathered.shape[3]
    table = beam_order(positions)
    flat = gathered.reshape(2 * NF, span_t * local)
    product = jnp.dot(table, flat, preferred_element_type=jnp.float32)
    real_part = product[:NF]
    imag_part = product[NF:]
    power = (real_part * real_part + imag_part * imag_part).reshape(NF, span_t, local)
    section_count = lax.axis_size("section")
    totals = lax.psum(jnp.sum(power, axis=1), "section")
    level = totals / (span_t * section_count)
    normed = power / (level[:, None, :] + EPSILON) - 1.0
    start = lax.axis_index("chan") * SUBCH + lax.axis_index("feed") * local
    delays = lax.dynamic_slice_in_dim(chan_delays, start, local, 1)
    partial = two_part_dot(normed.reshape(NF, span_t * local), channel_selector(delays, span_t))
    summed = lax.psum_scatter(partial, "feed", scatter_dimension=0, tiled=True)
    span_u = span_t + D1MAX
    blocks = summed.reshape(lax.axis_size("chan"), -1, span_u * NK)
    turned = lax.all_to_all(blocks, "chan", split_axis=0, concat_axis=0, tiled=True)
    bands, beams = turned.shape[0], turned.shape[1]
    subband = jnp.transpose(turned.reshape(bands, beams, span_u, NK), (1, 2, 0, 3))
    padded = jnp.pad(subband.reshape(beams, span_u, bands * NK), ((0, 0), (D2MAX, D2MAX), (0, 0)))
    span_v = span_u + D2MAX
    shifted = jnp.concatenate([padded[:, d : d + span_v] for d in range(D2MAX + 1)], axis=2)
    weights = subband_selector(sub_delays).reshape(-1, ND)
    dedispersed = two_part_dot(shifted.reshape(beams * span_v, -1), weights) * (1.0 / math.sqrt(C))
    dedispersed = dedispersed.reshape(beams, span_v, ND)
    later = lax.ppermute(dedispersed[:, :span_t], "section", [(1, 0)])
    extended = jnp.pad(dedispersed[:, BOXMAX:], ((0, 0), (0, BOXMAX), (0, 0)))
    extended = extended + jnp.pad(later, ((0, 0), (BOXMAX, 0), (0, 0)))
    return boxcar_filter(extended, boxcars, span_t)


def solution(mesh):
    return jax.shard_map(
        per_device,
        mesh=mesh,
        in_specs=(P(None, "feed", "section", "chan"), P(), P(), P(), P()),
        out_specs=P(("chan", "feed"), "section", None, None),
        check_vma=False,
    )
```

profile of v0, /device:TPU:1, one launch (start us, length us, event | category | flops | bytes accessed | tf_op | source)
XLA Modules:
  0.0 219.8 jit_solution(1089772544984727857)
XLA Ops:
  6.5 8.9 %copy.44 = bf16[2,256,12,256]{1,0,2,3:T(2,128)(2,1)} copy(bf16[2,256,12,256]{3,1,2,0:T(8,128)(2,1)} %param.5) | data formatting | bytes 6291456 | tf_op args[0]
  15.4 5.1 %all-to-all-start = ((bf16[2,256,12,256]{1,0,2,3:T(2,128)(2,1)}), bf16[2,256,12,256]{1,0,2,3:T(2,128)(2,1)}, u32[]{:S(2)}, u32[]{:S(2)}) async-start(bf16[2,256,12,256]{1,0,2,3:T(2,128)(2,1)} %copy.44), calls=%async_computation | async-start | bytes 6291456 | tf_op jit(solution)/shard_map/all_to_all | solution.py:73
  20.8 19.0 %fusion.14 = (bf16[1024,1024]{1,0:T(8,128)(2,1)S(1)}, bf16[1024,1024]{1,0:T(8,128)(2,1)}, bf16[1024,1024]{1,0:T(8,128)(2,1)}) fusion(s32[1024]{0:T(1024)S(1)} %copy-done.5, s32[1024]{0:T(1024)S(1)} %add.154), kind=kLoop, calls=%fused_computation.25 | loop fusion | flops 18874368 | bytes 6299648 | tf_op jit(solution)/shard_map/convert.5
  39.8 16.4 %all-to-all-done = bf16[2,256,12,256]{1,0,2,3:T(2,128)(2,1)} async-done(((bf16[2,256,12,256]{1,0,2,3:T(2,128)(2,1)}), bf16[2,256,12,256]{1,0,2,3:T(2,128)(2,1)}, u32[]{:S(2)}, u32[]{:S(2)}) %all-to-all-start) | async-done | bytes 3145760 | tf_op jit(solution)/shard_map/all_to_all | solution.py:73
  56.2 2.6 %copy.45 = bf16[2,256,12,256]{1,3,2,0:T(8,128)(2,1)S(1)} copy(bf16[2,256,12,256]{1,0,2,3:T(2,128)(2,1)} %all-to-all-done) | data formatting | bytes 6291456 | tf_op jit(solution)/shard_map/all_to_all | solution.py:73
  58.8 4.1 %copy.46 = bf16[2,4,256,12,64]{2,1,0,4,3:T(4,128)(2,1)} copy(bf16[2,4,256,12,64]{2,4,1,3,0:T(8,128)(2,1)S(1)} %bitcast.56) | data formatting | bytes 6291456 | tf_op jit(solution)/shard_map/all_to_all | solution.py:73
  62.9 6.1 %reshape.237 = bf16[2048,768]{0,1:T(8,128)(2,1)} reshape(bf16[2,4,256,12,64]{2,1,0,4,3:T(4,128)(2,1)} %copy.46) | data formatting | bytes 6291456 | tf_op jit(solution)/shard_map/reshape | solution.py:77
  69.0 16.8 %fusion = f32[2048,768]{0,1:T(8,128)S(1)} fusion(bf16[2048,768]{0,1:T(8,128)(2,1)} %reshape.237, bf16[1024,1024]{1,0:T(8,128)(2,1)} %get-tuple-element.16, bf16[1024,1024]{1,0:T(8,128)(2,1)} %get-tuple-element.15, bf16[1024,1024]{1,0:T(8,128)(2,1)S(1)} %get-tuple-element.14), kind=kOutput, calls=%fused_computation | convolution fusion | flops 6476005376 | bytes 15728640 | tf_op jit(solution)/shard_map/dot_general | solution.py:78
  85.9 2.8 %fusion.11 = f32[1024,768]{0,1:T(8,128)} fusion(f32[2048,768]{0,1:T(8,128)S(1)} %fusion), kind=kLoop, calls=%fused_computation.19 | loop fusion | flops 2359296 | bytes 9437184 | tf_op jit(solution)/shard_map/add | solution.py:81
  89.6 2.8 %reduce_sum.9 = f32[1024,64]{0,1:T(8,128)} reduce(f32[1024,12,64]{0,2,1:T(8,128)} %bitcast.57, f32[]{:T(128)} %constant.80.clone.1), dimensions={1}, to_apply=%region_0.1 | reduce | flops 720896 | bytes 3407876 | tf_op jit(solution)/shard_map/reduce_sum | solution.py:83
  93.8 32.2 %all-reduce.5.cloned.1.call-done = f32[1024,64]{0,1:T(8,128)} async-done(((f32[1024,64]{0,1:T(8,128)}), f32[1024,64]{0,1:T(8,128)}) %all-reduce.5.cloned.1.call-update) | async-done | bytes 262160 | tf_op jit(solution)/shard_map/psum | solution.py:83
  126.0 1.0 multiply_add_fusion
  126.9 3.6 %fusion.12 = f32[1024,768]{0,1:T(8,128)S(1)} fusion(f32[1024,64]{0,1:T(8,128)S(1)} %multiply_add_fusion, f32[2048,768]{0,1:T(8,128)} %copy-done.1), kind=kLoop, calls=%fused_computation.22 | loop fusion | flops 3932160 | bytes 9699328 | tf_op jit(solution)/shard_map/sub | solution.py:85
  131.1 1.5 fusion.16
  132.7 25.1 %reduce-scatter.2.cloned.1.call-done = f32[256,224]{0,1:T(8,128)} async-done(((f32[1024,224]{0,1:T(8,128)}), f32[256,224]{0,1:T(8,128)}) %reduce-scatter.2.cloned.1.call-update) | async-done | bytes 229392 | tf_op jit(solution)/shard_map/reduce_scatter | solution.py:89
  157.8 1.8 copy.47
  159.6 9.6 %all-to-all-start.1 = ((f32[32,8,224]{2,1,0:T(8,128)}), f32[32,8,224]{2,1,0:T(8,128)S(1)}, u32[]{:S(2)}, u32[]{:S(2)}) async-start(f32[32,8,224]{2,1,0:T(8,128)} %bitcast.5), calls=%async_computation.2 | async-start | bytes 524288 | tf_op jit(solution)/shard_map/all_to_all | solution.py:92
  169.2 1.2 broadcast_and_fusion
  170.4 9.2 %all-to-all-done.1 = f32[32,8,224]{2,1,0:T(8,128)S(1)} async-done(((f32[32,8,224]{2,1,0:T(8,128)}), f32[32,8,224]{2,1,0:T(8,128)S(1)}, u32[]{:S(2)}, u32[]{:S(2)}) %all-to-all-start.1) | async-done | bytes 229408 | tf_op jit(solution)/shard_map/all_to_all | solution.py:92
  180.5 1.3 reshape.241
  186.9 1.9 fusion.22
  188.8 2.4 %fusion.17 = f32[144,256]{1,0:T(8,128)S(1)} fusion(f32[144,256]{1,0:T(8,128)S(1)} %fusion.22, pred[2560,256]{1,0:T(8,128)(4,1)S(1)} %bitcast.60, f32[144,2560]{1,0:T(8,128)} %constant_dynamic-update-slice_fusion), kind=kOutput, calls=%fused_computation.31 | convolution fusion | flops 190291968 | bytes 2424832 | tf_op jit(solution)/shard_map/dot_general | solution.py:38
  191.2 5.7 %collective-permute-start = (f32[8,12,256]{2,1,0:T(8,128)S(1)}, f32[8,12,256]{2,1,0:T(8,128)S(1)}, u32[]{:S(2)}, u32[]{:S(2)}) collective-permute-start(f32[8,12,256]{2,1,0:T(8,128)S(1)} %get-tuple-element.12), channel_id=1, source_target_pairs={{128,0},{129,1},{130,2},{131,3},{132,4},{133,5},{134,6},{135,7},{1... | collective-permute-start | bytes 294920 | tf_op jit(solution)/shard_map/ppermute | solution.py:101
  212.1 0.9 copy.55
  (55 shorter events, 10.7 us)
Async XLA Ops:
  6.5 86.1 %copy-start = (s32[16,8192]{1,0:T(8,128)S(1)}, s32[16,8192]{1,0:T(8,128)}, u32[]{:S(2)}) copy-start(s32[16,8192]{1,0:T(8,128)} %param.7) | copy-start | bytes 1572868
  15.4 5.4 %copy-start.5 = (s32[1024]{0:T(1024)S(1)}, s32[1024]{0:T(1024)}, u32[]{:S(2)}) copy-start(s32[1024]{0:T(1024)} %param.6) | copy-start | bytes 12292
  15.4 40.8 %all-to-all-start = ((bf16[2,256,12,256]{1,0,2,3:T(2,128)(2,1)}), bf16[2,256,12,256]{1,0,2,3:T(2,128)(2,1)}, u32[]{:S(2)}, u32[]{:S(2)}) async-start(bf16[2,256,12,256]{1,0,2,3:T(2,128)(2,1)} %copy.44), calls=%async_computation | async-start | bytes 6291456 | tf_op jit(solution)/shard_map/all_to_all | solution.py:73
  20.5 105.4 %all-reduce.5.cloned.1.call-start = ((), (), s32[]{:S(2)}) async-start(), calls=%async_computation.3 | async-start | bytes 524288 | tf_op jit(solution)/shard_map/psum | solution.py:83
  85.9 3.7 %copy-start.1 = (f32[2048,768]{0,1:T(8,128)}, f32[2048,768]{0,1:T(8,128)S(1)}, u32[]{:S(2)}) copy-start(f32[2048,768]{0,1:T(8,128)S(1)} %fusion) | copy-start | bytes 18874372
  92.4 65.4 %reduce-scatter.2.cloned.1.call-start = ((), (), s32[]{:S(2)}) async-start(), calls=%async_computation.4 | async-start | bytes 1146880 | tf_op jit(solution)/shard_map/reduce_scatter | solution.py:89
  131.1 1.5 copy-start.3
  159.6 20.0 %all-to-all-start.1 = ((f32[32,8,224]{2,1,0:T(8,128)}), f32[32,8,224]{2,1,0:T(8,128)S(1)}, u32[]{:S(2)}, u32[]{:S(2)}) async-start(f32[32,8,224]{2,1,0:T(8,128)} %bitcast.5), calls=%async_computation.2 | async-start | bytes 524288 | tf_op jit(solution)/shard_map/all_to_all | solution.py:92
  183.2 3.7 %copy-start.2 = (pred[5,32,16,256]{3,2,1,0:T(8,128)(4,1)S(1)}, pred[5,32,16,256]{3,2,1,0:T(8,128)(4,1)}, u32[]{:S(2)}) copy-start(pred[5,32,16,256]{3,2,1,0:T(8,128)(4,1)} %broadcast_and_fusion) | copy-start | bytes 1966084
  186.9 10.0 %copy-start.4 = (s32[3,2]{0,1:T(2,128)S(1)}, s32[3,2]{0,1:T(2,128)}, u32[]{:S(2)}) copy-start(s32[3,2]{0,1:T(2,128)} %param.9) | copy-start | bytes 76
  191.2 19.8 %collective-permute-start = (f32[8,12,256]{2,1,0:T(8,128)S(1)}, f32[8,12,256]{2,1,0:T(8,128)S(1)}, u32[]{:S(2)}, u32[]{:S(2)}) collective-permute-start(f32[8,12,256]{2,1,0:T(8,128)S(1)} %get-tuple-element.12), channel_id=1, source_target_pairs={{128,0},{129,1},{130,2},{131,3},{132,4},{133,5},{134,6},{135,7},{1... | collective-permute-start | bytes 294920 | tf_op jit(solution)/shard_map/ppermute | solution.py:101
Sparse Core Ops, SparseCore 0:
  92.5 33.3 all-reduce.4
  132.7 25.0 reduce-scatter.1
where the time goes:
time: 221 us; the launch traced here: 220 us
  waiting for transfers between devices  82.9 us (38%)
  local copies, waits for them, and re-layouts  34 us (15%)
  other arithmetic  32.1 us (15%)
  between operations  27.2 us (12%)
  matrix products  23.1 us (10%)
  starting transfers between devices  20.6 us (9%)
    psum x1, waiting for transfers between devices, per_device(): totals = lax.psum(jnp.sum(power, axis=1), 'section')  32.2 us
    reduce_scatter x1, waiting for transfers between devices, per_device(): summed = lax.psum_scatter(partial, 'feed', scatter_dimension=0, tiled=True)  25.1 us
    another operation x1, other arithmetic  19 us
    dot_general x1, matrix products, per_device(): product = jnp.dot(table, flat, preferred_element_type=jnp.float32)  16.8 us
    all_to_all x1, waiting for transfers between devices, per_device(): lax.all_to_all(voltages, 'feed', split_axis=3, concat_axis=1, tiled=True)  16.4 us
    unnamed x17, local copies, waits for them, and re-layouts  12.7 us
    all_to_all x1, starting transfers between devices, per_device(): lax.all_to_all(blocks, 'chan', split_axis=0, concat_axis=0, tiled=True)  9.56 us
    all_to_all x1, waiting for transfers between devices, per_device(): lax.all_to_all(blocks, 'chan', split_axis=0, concat_axis=0, tiled=True)  9.17 us
  transfers between devices with their start and end apart: 5, of which 4 were waited for; matrix products, arithmetic and copies ran while one was open for 10% of the time, Pallas kernels for 0%

commit v1 on v0

v1 whole, which is shorter than its diff:
```python
import math

import jax
import jax.numpy as jnp
from jax import lax
from jax.experimental import pallas as pl
from jax.experimental.pallas import tpu as pltpu
from jax.sharding import PartitionSpec as P

NF = 1024
C = 8192
NK = 16
ND = 256
NW = 3
D1MAX = 2
D2MAX = 4
BOXMAX = 6
TT = 24
SUBCH = 256
EPSILON = 1e-05

SPAN = 12
LOCAL = 64
CHANS = 32
FEEDS = 4
CHUNKS = 3
SPAN_V = SPAN + BOXMAX
F32 = jnp.float32
BF16 = jnp.bfloat16
MESH = pl.DeviceIdType.MESH


def lane_ids(shape):
    return lax.broadcasted_iota(jnp.int32, shape, len(shape) - 1)


def row_ids(shape):
    return lax.broadcasted_iota(jnp.int32, shape, len(shape) - 2)


def kernel(
    v_ref, pos_ref, cd_ref, sd_ref, out_ref,
    vbuf, packed, arrived, relay_up, relay_down, table, acc, power,
    base_own, base_other, cdbuf, delay_t, chooser, weights,
    part_send, part_recv, block_send, block_recv, lhs, swap_send, swap_recv, trig,
    v_sem, cd_sem, a_send, a_recv, b_send, b_recv, p_send, p_recv, q_send, q_recv, s_send, s_recv,
):
    sec = lax.axis_index("section")
    ch = lax.axis_index("chan")
    fd = lax.axis_index("feed")
    up, down, far = lax.rem(fd + 1, 4), lax.rem(fd + 3, 4), lax.rem(fd + 2, 4)

    loads = []
    for j in range(CHUNKS):
        loads.append(
            pltpu.make_async_copy(v_ref.at[:, pl.ds(4 * j, 4)], vbuf.at[:, pl.ds(4 * j, 4)], v_sem.at[j])
        )
        loads[j].start()
    first = pl.multiple_of(ch * SUBCH, SUBCH)
    cd_load = pltpu.make_async_copy(cd_ref.at[:, pl.ds(first, SUBCH)], cdbuf, cd_sem)
    cd_load.start()

    barrier = pltpu.get_barrier_semaphore()
    for other in (up, down, far):
        pl.semaphore_signal(barrier, inc=1, device_id={"feed": other}, device_id_type=MESH)
    pl.semaphore_signal(barrier, inc=1, device_id={"section": 1 - sec}, device_id_type=MESH)

    @pl.loop(1, CHANS)
    def _(i):
        pl.semaphore_signal(
            barrier, inc=1, device_id={"chan": lax.rem(ch + i, CHANS)}, device_id_type=MESH
        )

    low_half = lane_ids((256, 128)) < LOCAL
    for j in range(CHUNKS):
        loads[j].wait()
        for part in range(2):
            for pair in range(2):
                for tile in range(2):
                    lanes = pl.ds(128 * tile, 128)
                    a = vbuf[part, 4 * j + 2 * pair, :, lanes]
                    b = vbuf[part, 4 * j + 2 * pair + 1, :, lanes]
                    even = jnp.where(low_half, a, pltpu.roll(b, LOCAL, 1))
                    odd = jnp.where(low_half, pltpu.roll(a, LOCAL, 1), b)
                    rows = pl.ds(256 * part, 256)
                    packed[2 * tile, j, rows, pl.ds(128 * pair, 128)] = even
                    packed[2 * tile + 1, j, rows, pl.ds(128 * pair, 128)] = odd

    pl.semaphore_wait(barrier, 3 + 1 + CHANS - 1)

    def to_feed(src, dst, sems, index, other):
        copy = pltpu.make_async_remote_copy(
            src_ref=src, dst_ref=dst, send_sem=sems[0].at[index], recv_sem=sems[1].at[index],
            device_id={"feed": other}, device_id_type=MESH,
        )
        copy.start()
        return copy

    a_sems = (a_send, a_recv)
    halves_up, halves_down, direct_up, direct_down, passed_up, passed_down = [], [], [], [], [], []
    re_rows, im_rows = pl.ds(0, 256), pl.ds(256, 256)
    for j in range(CHUNKS):
        halves_up.append(to_feed(packed.at[far, j, re_rows], relay_up.at[j], a_sems, 6 * j, up))
        halves_down.append(to_feed(packed.at[far, j, im_rows], relay_down.at[j], a_sems, 6 * j + 1, down))
    for j in range(CHUNKS):
        direct_up.append(to_feed(packed.at[up, j], arrived.at[j, 0], a_sems, 6 * j + 2, up))
        direct_down.append(to_feed(packed.at[down, j], arrived.at[j, 1], a_sems, 6 * j + 3, down))

    step = 2.0 * math.pi / NF
    for q, owner in enumerate((fd, down, up, far)):
        place = jnp.concatenate(
            [pos_ref[pl.ds(2 * owner, 1), :], pos_ref[pl.ds(2 * owner + 1, 1), :]], axis=1
        )
        ids = row_ids((32, 256))
        fine = ((ids * place) & (NF - 1)).astype(F32) * step
        coarse = ((ids * 32 * place) & (NF - 1)).astype(F32) * step
        trig[0] = jnp.cos(coarse)
        trig[1] = jnp.sin(coarse)
        trig[2] = jnp.cos(fine)
        trig[3] = jnp.sin(fine)

        @pl.loop(0, CHANS // 2)
        def _(i):
            cos_c = jnp.concatenate(
                [jnp.broadcast_to(trig[0, pl.ds(2 * i + n, 1), :], (8, 256)) for n in range(2)], axis=0
            )
            sin_c = jnp.concatenate(
                [jnp.broadcast_to(trig[1, pl.ds(2 * i + n, 1), :], (8, 256)) for n in range(2)], axis=0
            )
            for f in range(FEEDS):
                cos_f = jnp.concatenate([trig[2, 8 * f : 8 * f + 8, :]] * 2, axis=0)
                sin_f = jnp.concatenate([trig[3, 8 * f : 8 * f + 8, :]] * 2, axis=0)
                cosine = (cos_c * cos_f - sin_c * sin_f).astype(BF16)
                sine = sin_c * cos_f + cos_c * sin_f
                upper = pl.ds(pl.multiple_of(256 * f + 16 * i, 16), 16)
                lower = pl.ds(pl.multiple_of(NF + 256 * f + 16 * i, 16), 16)
                table[q, upper, 0:256] = cosine
                table[q, upper, 256:512] = sine.astype(BF16)
                table[q, lower, 0:256] = (-sine).astype(BF16)
                table[q, lower, 256:512] = cosine

    def block_dot(q, rows, right):
        return jnp.dot(table[q, rows, :], right, preferred_element_type=F32)

    for j in range(CHUNKS):
        @pl.loop(0, 4)
        def _(m):
            rows = pl.ds(pl.multiple_of(512 * m, 512), 512)
            acc[j, rows, :] = block_dot(0, rows, packed[fd, j])

    for j in range(CHUNKS):
        halves_up[j].wait_recv()
        passed_up.append(to_feed(relay_up.at[j], arrived.at[j, 2, re_rows], a_sems, 6 * j + 4, up))
        halves_down[j].wait_recv()
        passed_down.append(to_feed(relay_down.at[j], arrived.at[j, 2, im_rows], a_sems, 6 * j + 5, down))

    cd_load.wait()
    one_k = (row_ids((NK, 256)) == (lane_ids((NK, 256)) & (NK - 1))).astype(BF16)
    delay_t[...] = lax.dot_general(
        cdbuf[...].astype(F32).astype(BF16), one_k, (((0,), (0,)), ((), ())), preferred_element_type=F32
    )
    mine = delay_t[pl.ds(pl.multiple_of(fd * LOCAL, LOCAL), LOCAL), :]
    lanes = lane_ids((LOCAL, 256))
    turned = (lanes & 128) // 16 + (((lanes & 127) // 16 + 8 - lax.rem(ch, 8)) & 7)
    turned = turned.astype(F32)
    for t in range(SPAN):
        hit = (turned + mine) == float(t + D1MAX)
        chooser[LOCAL * t : LOCAL * (t + 1), :] = jnp.where(hit, 1.0, 0.0).astype(BF16)

    own_k = row_ids((NK, ND)) == lane_ids((NK, ND)) * NK // ND

    @pl.loop(0, CHANS)
    def _(s):
        delay = jnp.broadcast_to(sd_ref[pl.ds(s, 1), :], (NK, ND))
        rows = pl.ds(pl.multiple_of(NK * s, NK), NK)
        for d in range(D2MAX + 1):
            weights[d, rows, :] = jnp.where(own_k & (delay == d), 1.0, 0.0).astype(BF16)

    for j in range(CHUNKS):
        direct_up[j].wait_recv()
        direct_down[j].wait_recv()

        @pl.loop(0, 4)
        def _(m):
            rows = pl.ds(pl.multiple_of(512 * m, 512), 512)
            acc[j, rows, :] += block_dot(1, rows, arrived[j, 0]) + block_dot(2, rows, arrived[j, 1])

    def beam_power(j, f):
        rows = pl.ds(pl.multiple_of(256 * f, 256), 256)
        lower = pl.ds(pl.multiple_of(NF + 256 * f, 256), 256)
        right = arrived[j, 2]
        re = acc[j, rows, :] + block_dot(3, rows, right)
        im = acc[j, lower, :] + block_dot(3, lower, right)
        power[rows, 256 * j : 256 * (j + 1)] = re * re + im * im

    for j in range(CHUNKS):
        passed_up[j].wait_recv()
        passed_down[j].wait_recv()
        if j < CHUNKS - 1:
            @pl.loop(0, FEEDS)
            def _(f):
                beam_power(j, f)

    order = (far, up, down, fd)
    base_copies = []
    for n, f in enumerate(order):
        beam_power(CHUNKS - 1, f)
        rows = pl.ds(pl.multiple_of(256 * f, 256), 256)
        total = power[rows, 0:128]
        for tile in range(1, 6):
            total = total + power[rows, 128 * tile : 128 * (tile + 1)]
        base_own[n] = total + pltpu.roll(total, LOCAL, 1)
        copy = pltpu.make_async_remote_copy(
            src_ref=base_own.at[n], dst_ref=base_other.at[n], send_sem=b_send.at[n], recv_sem=b_recv.at[n],
            device_id={"section": 1 - sec}, device_id_type=MESH,
        )
        copy.start()
        base_copies.append(copy)

    part_copies = []
    own = None
    for n, f in enumerate(order):
        base_copies[n].wait_recv()
        rows = pl.ds(pl.multiple_of(256 * f, 256), 256)
        scale = 1.0 / ((base_own[n] + base_other[n]) * (1.0 / TT) + EPSILON)
        summed = None
        for tile in range(3):
            normed = jnp.concatenate(
                [power[rows, 256 * tile + 128 * h : 256 * tile + 128 * (h + 1)] * scale - 1.0 for h in range(2)],
                axis=1,
            )
            high = normed.astype(BF16)
            low = (normed - high.astype(F32)).astype(BF16)
            chosen = chooser[256 * tile : 256 * (tile + 1), :]
            term = jnp.dot(high, chosen, preferred_element_type=F32) + jnp.dot(
                low, chosen, preferred_element_type=F32
            )
            summed = term if summed is None else summed + term
        blocks = jnp.concatenate(
            [summed[:, 0:128].reshape(CHANS, 8, 128), summed[:, 128:256].reshape(CHANS, 8, 128)], axis=1
        )
        if n < 3:
            part_send[n] = blocks.astype(BF16)
            part_copies.append(to_feed(part_send.at[n], part_recv.at[n], (p_send, p_recv), n, f))
        else:
            own = blocks
    for copy in part_copies:
        copy.wait_recv()
    for n in range(3):
        own = own + part_recv[n].astype(F32)
    block_send[...] = own.astype(BF16)

    def chan_copy(i):
        other = lax.rem(ch + i, CHANS)
        return pltpu.make_async_remote_copy(
            src_ref=block_send.at[other], dst_ref=block_recv.at[ch],
            send_sem=q_send.at[other], recv_sem=q_recv.at[ch],
            device_id={"chan": other}, device_id_type=MESH,
        )

    @pl.loop(1, CHANS)
    def _(i):
        chan_copy(i).start()

    block_recv[ch] = block_send[ch]
    lhs[0:32, :] = jnp.zeros((32, 512), F32)
    lhs[144:176, :] = jnp.zeros((32, 512), F32)

    @pl.loop(1, CHANS)
    def _(i):
        other = lax.rem(ch + i, CHANS)
        pltpu.make_async_remote_copy(
            src_ref=block_send.at[other], dst_ref=block_recv.at[other],
            send_sem=q_send.at[other], recv_sem=q_recv.at[other],
            device_id={"chan": other}, device_id_type=MESH,
        ).wait_recv()

    spot = lane_ids((8, 128)) // 16
    for g in range(4):
        wide = [block_recv[8 * g + s].astype(F32) for s in range(8)]
        for u in range(SPAN + D1MAX):
            h = u // 8
            mixed = wide[0][8 * h : 8 * h + 8]
            for s in range(1, 8):
                mixed = jnp.where(spot == (u + s) % 8, wide[s][8 * h : 8 * h + 8], mixed)
            shift = (128 - 16 * (u % 8)) % 128
            if shift:
                mixed = pltpu.roll(mixed, shift, 1)
            lhs[32 + 8 * u : 40 + 8 * u, 128 * g : 128 * (g + 1)] = mixed

    found = None
    for d in range(D2MAX + 1):
        term = jnp.dot(lhs[8 * d : 8 * d + 8 * SPAN_V, :].astype(BF16), weights[d], preferred_element_type=F32)
        found = term if found is None else found + term
    found = found * (1.0 / math.sqrt(C))
    swap_send[...] = found[0 : 8 * SPAN]
    swap = pltpu.make_async_remote_copy(
        src_ref=swap_send, dst_ref=swap_recv, send_sem=s_send, recv_sem=s_recv,
        device_id={"section": 1 - sec}, device_id_type=MESH,
    )
    swap.start()
    out_ref[0 : 8 * SPAN, :] = found[8 * BOXMAX : 8 * SPAN_V]
    out_ref[8 * SPAN : 8 * SPAN_V, :] = jnp.zeros((8 * BOXMAX, ND), F32)
    swap.wait_recv()
    taken = jnp.where(jnp.full((8 * SPAN, ND), sec, jnp.int32) == 0, swap_recv[...], 0.0)
    out_ref[8 * BOXMAX : 8 * SPAN_V, :] += taken

    for group in (halves_up, halves_down, direct_up, direct_down, passed_up, passed_down):
        for copy in group:
            copy.wait_send()
    for copy in base_copies + part_copies:
        copy.wait_send()

    @pl.loop(1, CHANS)
    def _(i):
        chan_copy(i).wait_send()

    swap.wait_send()


def search(voltages, positions, chan_delays, sub_delays):
    vmem, anywhere = pl.BlockSpec(memory_space=pltpu.VMEM), pl.BlockSpec(memory_space=pl.ANY)
    dma = pltpu.SemaphoreType.DMA
    return pl.pallas_call(
        kernel,
        out_shape=jax.ShapeDtypeStruct((8 * SPAN_V, ND), F32),
        in_specs=[anywhere, vmem, anywhere, vmem],
        out_specs=vmem,
        scratch_shapes=[
            pltpu.VMEM((2, SPAN, 256, 256), BF16),
            pltpu.VMEM((4, CHUNKS, 512, 256), BF16),
            pltpu.VMEM((CHUNKS, 3, 512, 256), BF16),
            pltpu.VMEM((CHUNKS, 256, 256), BF16),
            pltpu.VMEM((CHUNKS, 256, 256), BF16),
            pltpu.VMEM((4, 2 * NF, 512), BF16),
            pltpu.VMEM((CHUNKS, 2 * NF, 256), F32),
            pltpu.VMEM((NF, SPAN * LOCAL), F32),
            pltpu.VMEM((4, 256, 128), F32),
            pltpu.VMEM((4, 256, 128), F32),
            pltpu.VMEM((NK, SUBCH), jnp.int32),
            pltpu.VMEM((SUBCH, 256), F32),
            pltpu.VMEM((SPAN * LOCAL, 256), BF16),
            pltpu.VMEM((D2MAX + 1, 512, ND), BF16),
            pltpu.VMEM((3, CHANS, 16, 128), BF16),
            pltpu.VMEM((3, CHANS, 16, 128), BF16),
            pltpu.VMEM((CHANS, 16, 128), BF16),
            pltpu.VMEM((CHANS, 16, 128), BF16),
            pltpu.VMEM((176, 512), F32),
            pltpu.VMEM((8 * SPAN, ND), F32),
            pltpu.VMEM((8 * SPAN, ND), F32),
            pltpu.VMEM((4, 32, 256), F32),
            dma((CHUNKS,)),
            dma,
            dma((6 * CHUNKS,)),
            dma((6 * CHUNKS,)),
            dma((4,)),
            dma((4,)),
            dma((3,)),
            dma((3,)),
            dma((CHANS,)),
            dma((CHANS,)),
            dma,
            dma,
        ],
        compiler_params=pltpu.CompilerParams(
            collective_id=0, has_side_effects=True, vmem_limit_bytes=60 * 1024 * 1024
        ),
        name="search",
    )(
        jnp.transpose(voltages, (0, 2, 1, 3)),
        positions.reshape(8, 128),
        chan_delays,
        jnp.transpose(sub_delays),
    )


def boxcar_filter(extended, boxcars):
    outputs = []
    for filter_index in range(NW):
        width_now = boxcars[filter_index, 0]
        stride_now = boxcars[filter_index, 1]
        summed = extended[:SPAN]
        for offset in range(1, NW + 1):
            start = jnp.minimum(offset * stride_now, BOXMAX)
            window_part = lax.dynamic_slice_in_dim(extended, start, SPAN, 0)
            summed = summed + jnp.where(offset < width_now, window_part, 0.0)
        outputs.append(summed * lax.rsqrt(width_now.astype(F32)))
    return jnp.transpose(jnp.stack(outputs, axis=1), (2, 0, 1, 3))


def per_device(voltages, positions, chan_delays, sub_delays, boxcars):
    extended = search(voltages, positions, chan_delays, sub_delays)
    return boxcar_filter(extended.reshape(SPAN_V, 8, ND), boxcars)


def solution(mesh):
    return jax.shard_map(
        per_device,
        mesh=mesh,
        in_specs=(P(None, "feed", "section", "chan"), P(), P(), P(), P()),
        out_specs=P(("chan", "feed"), "section", None, None),
        check_vma=False,
    )
```

time: 221 us -> 86.4 us (0.39)
  waiting for transfers between devices: 82.9 us -> 0 us
  Pallas kernels: 0 us -> 68.2 us
  local copies, waits for them, and re-layouts: 34 us -> 1.55 us
  other arithmetic: 32.1 us -> 3.16 us
  matrix products: 23.1 us -> 0 us
  starting transfers between devices: 20.6 us -> 0 us
  between operations: 27.2 us -> 13.1 us
    pallas_call x0 -> x1, Pallas kernels: none -> 68.2 us  [search(): pl.pallas_call(kernel, out_shape=jax.ShapeDtypeStruct((8 * SPAN_V, ND), F...]
    psum x1 -> x0, waiting for transfers between devices: 32.2 us -> none  [per_device(): totals = lax.psum(jnp.sum(power, axis=1), 'section')]
    all_to_all x2 -> x0, waiting for transfers between devices: 25.5 us -> none  [the longest x1 16.4 us: per_device(): lax.all_to_all(voltages, 'feed', split_axis=3, concat_axis=1, tiled=True)]
    reduce_scatter x1 -> x0, waiting for transfers between devices: 25.1 us -> none  [per_device(): summed = lax.psum_scatter(partial, 'feed', scatter_dimension=0, tiled=True)]
    dot_general x5 -> x0, matrix products: 23.1 us -> none  [the longest x1 16.8 us: per_device(): product = jnp.dot(table, flat, preferred_element_type=jnp.float32)]
    another operation x4 -> x2, other arithmetic: 20 us -> 2.42 us  [boxcar_filter(): return jnp.transpose(jnp.stack(outputs, axis=1), (2, 0, 1, 3))]
    all_to_all x2 -> x0, starting transfers between devices: 14.7 us -> none  [the longest x1 9.56 us: per_device(): lax.all_to_all(blocks, 'chan', split_axis=0, concat_axis=0, tiled=True)]
    unnamed x17 -> x0, local copies, waits for them, and re-layouts: 12.7 us -> none
  transfers between devices with their start and end apart: 5 -> 0, of which waited for: 4 -> 0; matrix products, arithmetic and copies ran while one was open for 10% -> 0% of each run, Pallas kernels for 0% -> 0%
where the time goes in v1:
time: 86.4 us; the launch traced here: 86 us
  Pallas kernels  68.2 us (79%)
  between operations  13.1 us (15%)
  other arithmetic  3.16 us (4%)
  local copies, waits for them, and re-layouts  1.55 us (2%)
    pallas_call x1, Pallas kernels, search(): pl.pallas_call(kernel, out_shape=jax.ShapeDtypeStruct((8 * SPAN_V, ND), F...  68.2 us
    another operation x2, other arithmetic, boxcar_filter(): return jnp.transpose(jnp.stack(outputs, axis=1), (2, 0, 1, 3))  2.42 us

profile of v1, /device:TPU:1, one launch (start us, length us, event | category | flops | bytes accessed | tf_op | source)
XLA Modules:
  0.0 86.0 jit_solution(10539655943308370936)
XLA Ops:
  0.0 1.6 %fusion.12 = (s32[1,1]{0,1:T(1,128)}, s32[1,1]{0,1:T(1,128)}, s32[1,1]{0,1:T(1,128)}, s32[1,1]{0,1:T(1,128)}, s32[1,1]{0,1:T(1,128)}, /*index=5*/s32[1,1]{0,1:T(1,128)}) fusion(s32[3,2]{0,1:T(2,128)} %param.9), kind=kLoop, calls=%fused_computation.16 | loop fusion | bytes 48 | tf_op jit(solution)/shard_map/slice | solution.py:380
  14.7 68.2 %search.1 = f32[144,256]{1,0:T(8,128)} custom-call(bf16[2,12,256,256]{3,2,1,0:T(8,128)(2,1)} %bitcast.67, s32[8,128]{1,0:T(8,128)} %bitcast.69, s32[16,8192]{1,0:T(8,128)} %cd_ref.1, s32[32,256]{1,0:T(8,128)} %bitcast.68), custom_call_target="tpu_custom_call" | custom-call | tf_op jit(solution)/shard_map/search/pallas_call | solution.py:324
  82.8 1.1 %fusion.7 = f32[12,1,8,256]{3,2,1,0:T(8,128)S(1)} fusion(f32[18,8,256]{2,1,0:T(8,128)} %bitcast.65, s32[]{:T(128)S(6)} %select_n.99, s32[]{:T(128)S(6)} %select_n.96, s32[]{:T(128)S(6)} %select_n.93, f32[144,256]{1,0:T(8,128)} %search.1, f32[]{:T(128)} %bitcast.20, pred[]{:T(512)} %bitcast.18, pred[]{:T(512)} %bitcast.16, pred[]{:T(512)} %bitcast.14), kind=kLoop, calls=%fused_computation.11 | loop fusion | flops 172032 | bytes 491539 | tf_op jit(solution)/shard_map/stack | solution.py:388
  84.0 1.3 %fusion.3 = (f32[12,1,8,256]{3,2,1,0:T(8,128)S(1)}, f32[12,1,8,256]{3,2,1,0:T(8,128)S(1)}) fusion(f32[18,8,256]{2,1,0:T(8,128)} %bitcast.66, s32[]{:T(128)S(6)} %select_n.90, s32[]{:T(128)S(6)} %select_n.87, s32[]{:T(128)S(6)} %select_n.84, f32[144,256]{1,0:T(8,128)} %search.1, f32[]{:T(128)} %bitcast.11, pred[]{:T(512)} %bitcast.9, pred[]{:T(512)} %bitcast.7, ...), kind=kLoop, calls=%fused_computation.7 | loop fusion | flops 344064 | bytes 884774 | tf_op jit(solution)/shard_map/stack | solution.py:388
  85.3 0.7 maximum_bitcast_fusion

commit v2 on v1

--- a/solution.py
+++ b/solution.py
@@ -374,18 +374,29 @@
     )
 
 
-def boxcar_filter(extended, boxcars):
-    outputs = []
+def boxcar_kernel(box_ref, ext_ref, out_ref):
     for filter_index in range(NW):
-        width_now = boxcars[filter_index, 0]
-        stride_now = boxcars[filter_index, 1]
-        summed = extended[:SPAN]
+        width_now = box_ref[0, filter_index]
+        stride_now = box_ref[1, filter_index]
+        gain = lax.rsqrt(jnp.full((8, ND), width_now, jnp.int32).astype(F32))
+        summed = ext_ref[0:SPAN]
         for offset in range(1, NW + 1):
             start = jnp.minimum(offset * stride_now, BOXMAX)
-            window_part = lax.dynamic_slice_in_dim(extended, start, SPAN, 0)
-            summed = summed + jnp.where(offset < width_now, window_part, 0.0)
-        outputs.append(summed * lax.rsqrt(width_now.astype(F32)))
-    return jnp.transpose(jnp.stack(outputs, axis=1), (2, 0, 1, 3))
+            kept = jnp.where(offset < width_now, 1.0, 0.0)
+            summed = summed + ext_ref[pl.ds(start, SPAN)] * kept
+        out_ref[:, filter_index] = summed * gain[None]
+
+
+def boxcar_filter(extended, boxcars):
+    vmem = pl.BlockSpec(memory_space=pltpu.VMEM)
+    filtered = pl.pallas_call(
+        boxcar_kernel,
+        out_shape=jax.ShapeDtypeStruct((SPAN, NW, 8, ND), F32),
+        in_specs=[pl.BlockSpec(memory_space=pltpu.SMEM), vmem],
+        out_specs=vmem,
+        name="boxcar",
+    )(jnp.transpose(boxcars), extended)
+    return jnp.transpose(filtered, (2, 0, 1, 3))
 
 
 def per_device(voltages, positions, chan_delays, sub_delays, boxcars):

time: 86.4 us -> 69.9 us (0.81)
  between operations: 13.1 us -> 0.01 us
  other arithmetic: 3.16 us -> 0 us
  Pallas kernels: 68.2 us -> 69.8 us
  local copies, waits for them, and re-layouts: 1.55 us -> 0 us
    another operation x2 -> x0, other arithmetic: 2.42 us -> none  [boxcar_filter(): return jnp.transpose(jnp.stack(outputs, axis=1), (2, 0, 1, 3))]
    pallas_call x0 -> x1, Pallas kernels: none -> 1.72 us  [boxcar_filter(): pl.pallas_call(boxcar_kernel, out_shape=jax.ShapeDtypeStruct((SPAN, NW, 8...]
    slice x1 -> x0, local copies, waits for them, and re-layouts: 1.55 us -> none  [boxcar_filter(): width_now = boxcars[filter_index, 0]]
where the time goes in v2:
time: 69.9 us; the launch traced here: 69.8 us
  Pallas kernels  69.8 us (100%)
    pallas_call x1, Pallas kernels, search(): pl.pallas_call(kernel, out_shape=jax.ShapeDtypeStruct((8 * SPAN_V, ND), F...  68 us
    pallas_call x1, Pallas kernels, boxcar_filter(): pl.pallas_call(boxcar_kernel, out_shape=jax.ShapeDtypeStruct((SPAN, NW, 8...  1.72 us

profile of v2, /device:TPU:1, one launch (start us, length us, event | category | flops | bytes accessed | tf_op | source)
XLA Modules:
  0.0 69.8 jit_solution(16761756453190664722)
XLA Ops:
  0.0 68.0 %search.1 = f32[144,256]{1,0:T(8,128)} custom-call(bf16[2,12,256,256]{3,2,1,0:T(8,128)(2,1)} %bitcast.6, s32[8,128]{1,0:T(8,128)} %bitcast.9, s32[16,8192]{1,0:T(8,128)} %cd_ref.1, s32[32,256]{1,0:T(8,128)} %bitcast.8), custom_call_target="tpu_custom_call" | custom-call | tf_op jit(solution)/shard_map/search/pallas_call | solution.py:324
  68.0 1.7 %boxcar.1 = f32[12,3,8,256]{3,2,1,0:T(8,128)} custom-call(s32[2,3]{1,0:T(2,128)} %bitcast.10, f32[18,8,256]{2,1,0:T(8,128)} %bitcast.7), custom_call_target="tpu_custom_call" | custom-call | tf_op jit(solution)/shard_map/boxcar/pallas_call | solution.py:392

commit v3 on v2

--- a/solution.py
+++ b/solution.py
@@ -41,13 +41,14 @@
 def kernel(
     v_ref, pos_ref, cd_ref, sd_ref, out_ref,
     vbuf, packed, arrived, relay_up, relay_down, table, acc, power,
-    base_own, base_other, cdbuf, delay_t, chooser, weights,
+    rim, base_own, base_other, cdbuf, delay_t, chooser, weights,
     part_send, part_recv, block_send, block_recv, lhs, swap_send, swap_recv, trig,
-    v_sem, cd_sem, a_send, a_recv, b_send, b_recv, p_send, p_recv, q_send, q_recv, s_send, s_recv,
+    v_sem, cd_sem, a_send, a_recv, r_send, r_recv, b_send, b_recv, p_send, p_recv, q_send, q_recv, s_send, s_recv,
 ):
     sec = lax.axis_index("section")
     ch = lax.axis_index("chan")
     fd = lax.axis_index("feed")
+    zed, ex = lax.div(ch, 4), lax.rem(ch, 4)
     up, down, far = lax.rem(fd + 1, 4), lax.rem(fd + 3, 4), lax.rem(fd + 2, 4)
 
     loads = []
@@ -121,19 +122,23 @@
 
         @pl.loop(0, CHANS // 2)
         def _(i):
+            hop = lax.div(i, 2)
+            pair = lax.rem(i, 2)
+            chan = lax.rem(zed + hop + 2, 8) * 4 + 2 * pair
+            base = lax.div(hop, 4) * 512 + lax.rem(hop, 4) * 32 + pair * 16
             cos_c = jnp.concatenate(
-                [jnp.broadcast_to(trig[0, pl.ds(2 * i + n, 1), :], (8, 256)) for n in range(2)], axis=0
+                [jnp.broadcast_to(trig[0, pl.ds(chan + n, 1), :], (8, 256)) for n in range(2)], axis=0
             )
             sin_c = jnp.concatenate(
-                [jnp.broadcast_to(trig[1, pl.ds(2 * i + n, 1), :], (8, 256)) for n in range(2)], axis=0
+                [jnp.broadcast_to(trig[1, pl.ds(chan + n, 1), :], (8, 256)) for n in range(2)], axis=0
             )
             for f in range(FEEDS):
                 cos_f = jnp.concatenate([trig[2, 8 * f : 8 * f + 8, :]] * 2, axis=0)
                 sin_f = jnp.concatenate([trig[3, 8 * f : 8 * f + 8, :]] * 2, axis=0)
                 cosine = (cos_c * cos_f - sin_c * sin_f).astype(BF16)
                 sine = sin_c * cos_f + cos_c * sin_f
-                upper = pl.ds(pl.multiple_of(256 * f + 16 * i, 16), 16)
-                lower = pl.ds(pl.multiple_of(NF + 256 * f + 16 * i, 16), 16)
+                upper = pl.ds(pl.multiple_of(128 * f + base, 16), 16)
+                lower = pl.ds(pl.multiple_of(NF + 128 * f + base, 16), 16)
                 table[q, upper, 0:256] = cosine
                 table[q, upper, 256:512] = sine.astype(BF16)
                 table[q, lower, 0:256] = (-sine).astype(BF16)
@@ -161,10 +166,13 @@
     )
     mine = delay_t[pl.ds(pl.multiple_of(fd * LOCAL, LOCAL), LOCAL), :]
     lanes = lane_ids((LOCAL, 256))
-    turned = (lanes & 128) // 16 + (((lanes & 127) // 16 + 8 - lax.rem(ch, 8)) & 7)
-    turned = turned.astype(F32)
-    for t in range(SPAN):
-        hit = (turned + mine) == float(t + D1MAX)
+    spot = (lanes & 127) // 16
+    early = (spot + 8 - lax.rem(ch, 8)) & 7
+    u_of = jnp.where(lanes < 128, early, 8 + (spot & 3)).astype(F32)
+    for t in range(SPAN + D1MAX):
+        hit = (u_of + mine) == float(t)
+        if t >= SPAN:
+            hit = hit & (jnp.full((LOCAL, 256), sec, jnp.int32) == 0)
         chooser[LOCAL * t : LOCAL * (t + 1), :] = jnp.where(hit, 1.0, 0.0).astype(BF16)
 
     own_k = row_ids((NK, ND)) == lane_ids((NK, ND)) * NK // ND
@@ -185,136 +193,163 @@
             rows = pl.ds(pl.multiple_of(512 * m, 512), 512)
             acc[j, rows, :] += block_dot(1, rows, arrived[j, 0]) + block_dot(2, rows, arrived[j, 1])
 
-    def beam_power(j, f):
-        rows = pl.ds(pl.multiple_of(256 * f, 256), 256)
-        lower = pl.ds(pl.multiple_of(NF + 256 * f, 256), 256)
+    def beam_power(j, m):
+        rows = pl.ds(pl.multiple_of(512 * m, 512), 512)
+        lower = pl.ds(pl.multiple_of(NF + 512 * m, 512), 512)
         right = arrived[j, 2]
         re = acc[j, rows, :] + block_dot(3, rows, right)
         im = acc[j, lower, :] + block_dot(3, lower, right)
         power[rows, 256 * j : 256 * (j + 1)] = re * re + im * im
 
-    for j in range(CHUNKS):
+    def to_core(src, dst, send_sem, recv_sem):
+        copy = pltpu.make_async_remote_copy(
+            src_ref=src, dst_ref=dst, send_sem=send_sem, recv_sem=recv_sem,
+            device_id={"section": 1 - sec}, device_id_type=MESH,
+        )
+        copy.start()
+        return copy
+
+    rim_copy = None
+    for j in range(CHUNKS - 1):
         passed_up[j].wait_recv()
         passed_down[j].wait_recv()
-        if j < CHUNKS - 1:
-            @pl.loop(0, FEEDS)
-            def _(f):
-                beam_power(j, f)
-
-    order = (far, up, down, fd)
+
+        @pl.loop(0, 2)
+        def _(m):
+            beam_power(j, m)
+
+        if j == 0:
+            rim_copy = to_core(power.at[:, pl.ds(0, 128)], rim, r_send, r_recv)
+
+    passed_up[CHUNKS - 1].wait_recv()
+    passed_down[CHUNKS - 1].wait_recv()
     base_copies = []
-    for n, f in enumerate(order):
-        beam_power(CHUNKS - 1, f)
-        rows = pl.ds(pl.multiple_of(256 * f, 256), 256)
+    for h in range(2):
+        beam_power(CHUNKS - 1, h)
+        rows = pl.ds(512 * h, 512)
         total = power[rows, 0:128]
         for tile in range(1, 6):
             total = total + power[rows, 128 * tile : 128 * (tile + 1)]
-        base_own[n] = total + pltpu.roll(total, LOCAL, 1)
-        copy = pltpu.make_async_remote_copy(
-            src_ref=base_own.at[n], dst_ref=base_other.at[n], send_sem=b_send.at[n], recv_sem=b_recv.at[n],
-            device_id={"section": 1 - sec}, device_id_type=MESH,
-        )
-        copy.start()
-        base_copies.append(copy)
-
-    part_copies = []
-    own = None
-    for n, f in enumerate(order):
-        base_copies[n].wait_recv()
-        rows = pl.ds(pl.multiple_of(256 * f, 256), 256)
-        scale = 1.0 / ((base_own[n] + base_other[n]) * (1.0 / TT) + EPSILON)
-        summed = None
-        for tile in range(3):
-            normed = jnp.concatenate(
-                [power[rows, 256 * tile + 128 * h : 256 * tile + 128 * (h + 1)] * scale - 1.0 for h in range(2)],
-                axis=1,
-            )
-            high = normed.astype(BF16)
-            low = (normed - high.astype(F32)).astype(BF16)
-            chosen = chooser[256 * tile : 256 * (tile + 1), :]
-            term = jnp.dot(high, chosen, preferred_element_type=F32) + jnp.dot(
-                low, chosen, preferred_element_type=F32
-            )
-            summed = term if summed is None else summed + term
-        blocks = jnp.concatenate(
-            [summed[:, 0:128].reshape(CHANS, 8, 128), summed[:, 128:256].reshape(CHANS, 8, 128)], axis=1
-        )
-        if n < 3:
-            part_send[n] = blocks.astype(BF16)
-            part_copies.append(to_feed(part_send.at[n], part_recv.at[n], (p_send, p_recv), n, f))
-        else:
-            own = blocks
-    for copy in part_copies:
-        copy.wait_recv()
-    for n in range(3):
-        own = own + part_recv[n].astype(F32)
-    block_send[...] = own.astype(BF16)
-
-    def chan_copy(i):
-        other = lax.rem(ch + i, CHANS)
-        return pltpu.make_async_remote_copy(
-            src_ref=block_send.at[other], dst_ref=block_recv.at[ch],
-            send_sem=q_send.at[other], recv_sem=q_recv.at[ch],
-            device_id={"chan": other}, device_id_type=MESH,
-        )
-
-    @pl.loop(1, CHANS)
-    def _(i):
-        chan_copy(i).start()
-
-    block_recv[ch] = block_send[ch]
+        base_own[h] = total + pltpu.roll(total, LOCAL, 1)
+        base_copies.append(to_core(base_own.at[h], base_other.at[h], b_send.at[h], b_recv.at[h]))
+
+    rim_copy.wait_recv()
+    low_lanes = lane_ids((2, 4, 2, 8, 128)) < LOCAL
+    part_copies, owns = [], []
+    for h in range(2):
+        base_copies[h].wait_recv()
+        copies = []
+        for pair in ((far, up), (down, fd)):
+            tiles = [[] for _ in range(7)]
+            for f in pair:
+                within = pl.ds(pl.multiple_of(128 * f, 128), 128)
+                rows = pl.ds(pl.multiple_of(512 * h + 128 * f, 128), 128)
+                scale = 1.0 / ((base_own[h, within] + base_other[h, within]) * (1.0 / TT) + EPSILON)
+                for tile in range(7):
+                    part = power[rows, 128 * tile : 128 * (tile + 1)] if tile < 6 else rim[rows, :]
+                    tiles[tile].append(part * scale - 1.0)
+            tiles = [jnp.concatenate(parts, axis=0) for parts in tiles]
+            summed = None
+            for tile in range(4):
+                normed = jnp.concatenate(tiles[2 * tile : 2 * tile + 2], axis=1)
+                high = normed.astype(BF16)
+                low = (normed - high.astype(F32)).astype(BF16)
+                chosen = chooser[256 * tile : 256 * tile + normed.shape[1], :]
+                term = jnp.dot(jnp.concatenate([high, low], axis=0), chosen, preferred_element_type=F32)
+                summed = term if summed is None else summed + term
+            summed = summed[0:256] + summed[256:512]
+            early = summed[:, 0:128].reshape(2, 4, 32, 128)
+            late = summed[:, 128:256].reshape(2, 4, 2, 2, 8, 128)
+            late = jnp.where(low_lanes, late[:, :, :, 0], late[:, :, :, 1]).reshape(2, 4, 16, 128)
+            blocks = jnp.concatenate([early, late], axis=2)
+            for a in range(2):
+                n = len(copies)
+                if n < 3:
+                    part_send[h, n] = blocks[a].astype(BF16)
+                    copies.append(
+                        to_feed(part_send.at[h, n], part_recv.at[h, n], (p_send, p_recv), 3 * h + n, pair[a])
+                    )
+                else:
+                    owns.append(blocks[a])
+        part_copies.append(copies)
+
+    chan_copies = []
+    for h in range(2):
+        total = owns[h]
+        for n in range(3):
+            part_copies[h][n].wait_recv()
+            total = total + part_recv[h, n].astype(F32)
+        for x in range(4):
+            late = total[:, 32 + 8 * (x // 2) : 40 + 8 * (x // 2)].reshape(32, 128)
+            if x % 2:
+                late = pltpu.roll(late, LOCAL, 1)
+            block = jnp.concatenate([total[:, 8 * x : 8 * x + 8], late.reshape(4, 8, 128)], axis=1)
+            block_send[4 * h : 4 * h + 4, x] = block.astype(BF16)
+        for a in range(4):
+            hop = (4 * h + a + 2) % 8
+            for i in ((2, 1, 3) if hop == 0 else (2, 1, 3, 0)):
+                x = lax.rem(ex + i, 4)
+                other = lax.rem(zed + hop, 8) * 4 + x
+                copy = pltpu.make_async_remote_copy(
+                    src_ref=block_send.at[4 * h + a, x], dst_ref=block_recv.at[ch],
+                    send_sem=q_send.at[4 * (4 * h + a) + i], recv_sem=q_recv.at[ch],
+                    device_id={"chan": other}, device_id_type=MESH,
+                )
+                copy.start()
+                chan_copies.append(copy)
+
+    block_recv[ch] = block_send[6, ex]
     lhs[0:32, :] = jnp.zeros((32, 512), F32)
-    lhs[144:176, :] = jnp.zeros((32, 512), F32)
+    lhs[128:160, :] = jnp.zeros((32, 512), F32)
 
     @pl.loop(1, CHANS)
     def _(i):
         other = lax.rem(ch + i, CHANS)
         pltpu.make_async_remote_copy(
-            src_ref=block_send.at[other], dst_ref=block_recv.at[other],
-            send_sem=q_send.at[other], recv_sem=q_recv.at[other],
+            src_ref=block_send.at[0, 0], dst_ref=block_recv.at[other],
+            send_sem=q_send.at[0], recv_sem=q_recv.at[other],
             device_id={"chan": other}, device_id_type=MESH,
         ).wait_recv()
 
     spot = lane_ids((8, 128)) // 16
     for g in range(4):
         wide = [block_recv[8 * g + s].astype(F32) for s in range(8)]
-        for u in range(SPAN + D1MAX):
-            h = u // 8
-            mixed = wide[0][8 * h : 8 * h + 8]
-            for s in range(1, 8):
-                mixed = jnp.where(spot == (u + s) % 8, wide[s][8 * h : 8 * h + 8], mixed)
-            shift = (128 - 16 * (u % 8)) % 128
-            if shift:
-                mixed = pltpu.roll(mixed, shift, 1)
+        for u in range(SPAN):
+            if u < 8:
+                mixed = wide[0][0:8]
+                for s in range(1, 8):
+                    mixed = jnp.where(spot == (u + s) % 8, wide[s][0:8], mixed)
+                if u:
+                    mixed = pltpu.roll(mixed, 128 - 16 * u, 1)
+            else:
+                mixed = None
+                for s in range(8):
+                    shift = (16 * (s - (u - 8))) % 128
+                    moved = pltpu.roll(wide[s][8:16], shift, 1) if shift else wide[s][8:16]
+                    mixed = moved if mixed is None else jnp.where(spot == s, moved, mixed)
             lhs[32 + 8 * u : 40 + 8 * u, 128 * g : 128 * (g + 1)] = mixed
 
     found = None
     for d in range(D2MAX + 1):
-        term = jnp.dot(lhs[8 * d : 8 * d + 8 * SPAN_V, :].astype(BF16), weights[d], preferred_element_type=F32)
+        term = jnp.dot(lhs[8 * d : 8 * d + 128, :].astype(BF16), weights[d], preferred_element_type=F32)
         found = term if found is None else found + term
     found = found * (1.0 / math.sqrt(C))
-    swap_send[...] = found[0 : 8 * SPAN]
-    swap = pltpu.make_async_remote_copy(
-        src_ref=swap_send, dst_ref=swap_recv, send_sem=s_send, recv_sem=s_recv,
-        device_id={"section": 1 - sec}, device_id_type=MESH,
-    )
-    swap.start()
-    out_ref[0 : 8 * SPAN, :] = found[8 * BOXMAX : 8 * SPAN_V]
+    swap_send[...] = found[0:80]
+    swap = to_core(swap_send, swap_recv, s_send, s_recv)
+    out_ref[0 : 8 * SPAN, :] = found[32:128]
     out_ref[8 * SPAN : 8 * SPAN_V, :] = jnp.zeros((8 * BOXMAX, ND), F32)
     swap.wait_recv()
-    taken = jnp.where(jnp.full((8 * SPAN, ND), sec, jnp.int32) == 0, swap_recv[...], 0.0)
-    out_ref[8 * BOXMAX : 8 * SPAN_V, :] += taken
+    taken = jnp.where(jnp.full((80, ND), sec, jnp.int32) == 0, swap_recv[...], 0.0)
+    out_ref[64 : 8 * SPAN_V, :] += taken
 
     for group in (halves_up, halves_down, direct_up, direct_down, passed_up, passed_down):
         for copy in group:
             copy.wait_send()
-    for copy in base_copies + part_copies:
+    for copy in base_copies + part_copies[0] + part_copies[1]:
         copy.wait_send()
-
-    @pl.loop(1, CHANS)
-    def _(i):
-        chan_copy(i).wait_send()
-
+    for copy in chan_copies:
+        copy.wait_send()
+    rim_copy.wait_send()
     swap.wait_send()
 
 
@@ -335,28 +370,31 @@
             pltpu.VMEM((4, 2 * NF, 512), BF16),
             pltpu.VMEM((CHUNKS, 2 * NF, 256), F32),
             pltpu.VMEM((NF, SPAN * LOCAL), F32),
-            pltpu.VMEM((4, 256, 128), F32),
-            pltpu.VMEM((4, 256, 128), F32),
+            pltpu.VMEM((NF, 128), F32),
+            pltpu.VMEM((2, 512, 128), F32),
+            pltpu.VMEM((2, 512, 128), F32),
             pltpu.VMEM((NK, SUBCH), jnp.int32),
             pltpu.VMEM((SUBCH, 256), F32),
-            pltpu.VMEM((SPAN * LOCAL, 256), BF16),
+            pltpu.VMEM(((SPAN + D1MAX) * LOCAL, 256), BF16),
             pltpu.VMEM((D2MAX + 1, 512, ND), BF16),
-            pltpu.VMEM((3, CHANS, 16, 128), BF16),
-            pltpu.VMEM((3, CHANS, 16, 128), BF16),
+            pltpu.VMEM((2, 3, 4, 48, 128), BF16),
+            pltpu.VMEM((2, 3, 4, 48, 128), BF16),
+            pltpu.VMEM((8, 4, 16, 128), BF16),
             pltpu.VMEM((CHANS, 16, 128), BF16),
-            pltpu.VMEM((CHANS, 16, 128), BF16),
-            pltpu.VMEM((176, 512), F32),
-            pltpu.VMEM((8 * SPAN, ND), F32),
-            pltpu.VMEM((8 * SPAN, ND), F32),
+            pltpu.VMEM((160, 512), F32),
+            pltpu.VMEM((80, ND), F32),
+            pltpu.VMEM((80, ND), F32),
             pltpu.VMEM((4, 32, 256), F32),
             dma((CHUNKS,)),
             dma,
             dma((6 * CHUNKS,)),
             dma((6 * CHUNKS,)),
-            dma((4,)),
-            dma((4,)),
-            dma((3,)),
-            dma((3,)),
+            dma,
+            dma,
+            dma((2,)),
+            dma((2,)),
+            dma((6,)),
+            dma((6,)),
             dma((CHANS,)),
             dma((CHANS,)),
             dma,

time: 69.9 us -> 66.8 us (0.956)
  Pallas kernels: 69.8 us -> 66.6 us
    pallas_call x1, Pallas kernels: 68 us -> 64.9 us  [search(): pl.pallas_call(kernel, out_shape=jax.ShapeDtypeStruct((8 * SPAN_V, ND), F...]
where the time goes in v3:
time: 66.8 us; the launch traced here: 66.6 us
  Pallas kernels  66.6 us (100%)
    pallas_call x1, Pallas kernels, search(): pl.pallas_call(kernel, out_shape=jax.ShapeDtypeStruct((8 * SPAN_V, ND), F...  64.9 us
    pallas_call x1, Pallas kernels, boxcar_filter(): pl.pallas_call(boxcar_kernel, out_shape=jax.ShapeDtypeStruct((SPAN, NW, 8...  1.72 us

profile of v3, /device:TPU:1, one launch (start us, length us, event | category | flops | bytes accessed | tf_op | source)
XLA Modules:
  0.0 66.6 jit_solution(9129050856977981529)
XLA Ops:
  0.0 64.9 %search.1 = f32[144,256]{1,0:T(8,128)} custom-call(bf16[2,12,256,256]{3,2,1,0:T(8,128)(2,1)} %bitcast.6, s32[8,128]{1,0:T(8,128)} %bitcast.9, s32[16,8192]{1,0:T(8,128)} %cd_ref.1, s32[32,256]{1,0:T(8,128)} %bitcast.8), custom_call_target="tpu_custom_call" | custom-call | tf_op jit(solution)/shard_map/search/pallas_call | solution.py:359
  64.9 1.7 %boxcar.1 = f32[12,3,8,256]{3,2,1,0:T(8,128)} custom-call(s32[2,3]{1,0:T(2,128)} %bitcast.10, f32[18,8,256]{2,1,0:T(8,128)} %bitcast.7), custom_call_target="tpu_custom_call" | custom-call | tf_op jit(solution)/shard_map/boxcar/pallas_call | solution.py:430

commit v4 on v3

--- a/solution.py
+++ b/solution.py
@@ -39,11 +39,11 @@
 
 
 def kernel(
-    v_ref, pos_ref, cd_ref, sd_ref, out_ref,
-    vbuf, packed, arrived, relay_up, relay_down, table, acc, power,
+    v_ref, pos_any, cd_ref, sd_any, out_ref,
+    pos_ref, sd_ref, vbuf, packed, arrived, relay_up, relay_down, table, acc, power,
     rim, base_own, base_other, cdbuf, delay_t, chooser, weights,
-    part_send, part_recv, block_send, block_recv, lhs, swap_send, swap_recv, trig,
-    v_sem, cd_sem, a_send, a_recv, r_send, r_recv, b_send, b_recv, p_send, p_recv, q_send, q_recv, s_send, s_recv,
+    part_own, part_send, part_recv, block_send, block_recv, lhs, swap_send, swap_recv, trig,
+    v_sem, cd_sem, pos_sem, sd_sem, a_send, a_recv, r_send, r_recv, b_send, b_recv, p_send, p_recv, q_send, q_recv, s_send, s_recv,
 ):
     sec = lax.axis_index("section")
     ch = lax.axis_index("chan")
@@ -51,6 +51,17 @@
     zed, ex = lax.div(ch, 4), lax.rem(ch, 4)
     up, down, far = lax.rem(fd + 1, 4), lax.rem(fd + 3, 4), lax.rem(fd + 2, 4)
 
+    barrier = pltpu.get_barrier_semaphore()
+    for other in (up, down, far):
+        pl.semaphore_signal(barrier, inc=1, device_id={"feed": other}, device_id_type=MESH)
+    pl.semaphore_signal(barrier, inc=1, device_id={"section": 1 - sec}, device_id_type=MESH)
+
+    @pl.loop(1, CHANS)
+    def _(i):
+        pl.semaphore_signal(
+            barrier, inc=1, device_id={"chan": lax.rem(ch + i, CHANS)}, device_id_type=MESH
+        )
+
     loads = []
     for j in range(CHUNKS):
         loads.append(
@@ -60,17 +71,10 @@
     first = pl.multiple_of(ch * SUBCH, SUBCH)
     cd_load = pltpu.make_async_copy(cd_ref.at[:, pl.ds(first, SUBCH)], cdbuf, cd_sem)
     cd_load.start()
-
-    barrier = pltpu.get_barrier_semaphore()
-    for other in (up, down, far):
-        pl.semaphore_signal(barrier, inc=1, device_id={"feed": other}, device_id_type=MESH)
-    pl.semaphore_signal(barrier, inc=1, device_id={"section": 1 - sec}, device_id_type=MESH)
-
-    @pl.loop(1, CHANS)
-    def _(i):
-        pl.semaphore_signal(
-            barrier, inc=1, device_id={"chan": lax.rem(ch + i, CHANS)}, device_id_type=MESH
-        )
+    pos_load = pltpu.make_async_copy(pos_any, pos_ref, pos_sem)
+    pos_load.start()
+    sd_load = pltpu.make_async_copy(sd_any, sd_ref, sd_sem)
+    sd_load.start()
 
     low_half = lane_ids((256, 128)) < LOCAL
     for j in range(CHUNKS):
@@ -108,6 +112,7 @@
         direct_down.append(to_feed(packed.at[down, j], arrived.at[j, 1], a_sems, 6 * j + 3, down))
 
     step = 2.0 * math.pi / NF
+    pos_load.wait()
     for q, owner in enumerate((fd, down, up, far)):
         place = jnp.concatenate(
             [pos_ref[pl.ds(2 * owner, 1), :], pos_ref[pl.ds(2 * owner + 1, 1), :]], axis=1
@@ -124,8 +129,8 @@
         def _(i):
             hop = lax.div(i, 2)
             pair = lax.rem(i, 2)
-            chan = lax.rem(zed + hop + 2, 8) * 4 + 2 * pair
-            base = lax.div(hop, 4) * 512 + lax.rem(hop, 4) * 32 + pair * 16
+            chan = lax.rem(zed + hop + 3, 8) * 4 + 2 * pair
+            base = lax.div(hop, 2) * 256 + lax.rem(hop, 2) * 32 + pair * 16
             cos_c = jnp.concatenate(
                 [jnp.broadcast_to(trig[0, pl.ds(chan + n, 1), :], (8, 256)) for n in range(2)], axis=0
             )
@@ -137,8 +142,8 @@
                 sin_f = jnp.concatenate([trig[3, 8 * f : 8 * f + 8, :]] * 2, axis=0)
                 cosine = (cos_c * cos_f - sin_c * sin_f).astype(BF16)
                 sine = sin_c * cos_f + cos_c * sin_f
-                upper = pl.ds(pl.multiple_of(128 * f + base, 16), 16)
-                lower = pl.ds(pl.multiple_of(NF + 128 * f + base, 16), 16)
+                upper = pl.ds(pl.multiple_of(64 * f + base, 16), 16)
+                lower = pl.ds(pl.multiple_of(NF + 64 * f + base, 16), 16)
                 table[q, upper, 0:256] = cosine
                 table[q, upper, 256:512] = sine.astype(BF16)
                 table[q, lower, 0:256] = (-sine).astype(BF16)
@@ -175,6 +180,7 @@
             hit = hit & (jnp.full((LOCAL, 256), sec, jnp.int32) == 0)
         chooser[LOCAL * t : LOCAL * (t + 1), :] = jnp.where(hit, 1.0, 0.0).astype(BF16)
 
+    sd_load.wait()
     own_k = row_ids((NK, ND)) == lane_ids((NK, ND)) * NK // ND
 
     @pl.loop(0, CHANS)
@@ -234,73 +240,68 @@
         base_copies.append(to_core(base_own.at[h], base_other.at[h], b_send.at[h], b_recv.at[h]))
 
     rim_copy.wait_recv()
-    low_lanes = lane_ids((2, 4, 2, 8, 128)) < LOCAL
-    part_copies, owns = [], []
-    for h in range(2):
-        base_copies[h].wait_recv()
-        copies = []
-        for pair in ((far, up), (down, fd)):
-            tiles = [[] for _ in range(7)]
-            for f in pair:
-                within = pl.ds(pl.multiple_of(128 * f, 128), 128)
-                rows = pl.ds(pl.multiple_of(512 * h + 128 * f, 128), 128)
-                scale = 1.0 / ((base_own[h, within] + base_other[h, within]) * (1.0 / TT) + EPSILON)
-                for tile in range(7):
-                    part = power[rows, 128 * tile : 128 * (tile + 1)] if tile < 6 else rim[rows, :]
-                    tiles[tile].append(part * scale - 1.0)
-            tiles = [jnp.concatenate(parts, axis=0) for parts in tiles]
-            summed = None
-            for tile in range(4):
-                normed = jnp.concatenate(tiles[2 * tile : 2 * tile + 2], axis=1)
-                high = normed.astype(BF16)
-                low = (normed - high.astype(F32)).astype(BF16)
-                chosen = chooser[256 * tile : 256 * tile + normed.shape[1], :]
-                term = jnp.dot(jnp.concatenate([high, low], axis=0), chosen, preferred_element_type=F32)
-                summed = term if summed is None else summed + term
-            summed = summed[0:256] + summed[256:512]
-            early = summed[:, 0:128].reshape(2, 4, 32, 128)
-            late = summed[:, 128:256].reshape(2, 4, 2, 2, 8, 128)
-            late = jnp.where(low_lanes, late[:, :, :, 0], late[:, :, :, 1]).reshape(2, 4, 16, 128)
-            blocks = jnp.concatenate([early, late], axis=2)
-            for a in range(2):
-                n = len(copies)
-                if n < 3:
-                    part_send[h, n] = blocks[a].astype(BF16)
-                    copies.append(
-                        to_feed(part_send.at[h, n], part_recv.at[h, n], (p_send, p_recv), 3 * h + n, pair[a])
-                    )
-                else:
-                    owns.append(blocks[a])
-        part_copies.append(copies)
+    low_lanes = lane_ids((4, 2, 2, 8, 128)) < LOCAL
+    part_copies = {}
+    turns = (0, 1, 3, 2)
+    for q in turns:
+        h = q // 2
+        if q in (0, 3):
+            base_copies[h].wait_recv()
+        within = pl.ds(256 * (q % 2), 256)
+        rows = pl.ds(256 * q, 256)
+        scale = 1.0 / ((base_own[h, within] + base_other[h, within]) * (1.0 / TT) + EPSILON)
+        tiles = [power[rows, 128 * tile : 128 * (tile + 1)] * scale - 1.0 for tile in range(6)]
+        tiles.append(rim[rows, :] * scale - 1.0)
+        summed = None
+        for tile in range(4):
+            normed = jnp.concatenate(tiles[2 * tile : 2 * tile + 2], axis=1)
+            high = normed.astype(BF16)
+            low = (normed - high.astype(F32)).astype(BF16)
+            chosen = chooser[256 * tile : 256 * tile + normed.shape[1], :]
+            term = jnp.dot(jnp.concatenate([high, low], axis=0), chosen, preferred_element_type=F32)
+            summed = term if summed is None else summed + term
+        summed = summed[0:256] + summed[256:512]
+        early = summed[:, 0:128].reshape(4, 2, 32, 128)
+        late = summed[:, 128:256].reshape(4, 2, 2, 2, 8, 128)
+        late = jnp.where(low_lanes, late[:, :, :, 0], late[:, :, :, 1]).reshape(4, 2, 16, 128)
+        blocks = jnp.concatenate([early, late], axis=2)
+        part_own[q] = blocks
+        part_send[q] = blocks.astype(BF16)
+        part_copies[q] = [
+            to_feed(part_send.at[q, f], part_recv.at[q, n], (p_send, p_recv), 3 * q + n, f)
+            for n, f in enumerate((far, up, down))
+        ]
+
+    lhs[0:32, :] = jnp.zeros((32, 512), F32)
+    lhs[128:160, :] = jnp.zeros((32, 512), F32)
 
     chan_copies = []
-    for h in range(2):
-        total = owns[h]
+    for q in turns:
+        total = part_own[q, fd]
         for n in range(3):
-            part_copies[h][n].wait_recv()
-            total = total + part_recv[h, n].astype(F32)
+            part_copies[q][n].wait_recv()
+            total = total + part_recv[q, n].astype(F32)
         for x in range(4):
-            late = total[:, 32 + 8 * (x // 2) : 40 + 8 * (x // 2)].reshape(32, 128)
+            late = total[:, 32 + 8 * (x // 2) : 40 + 8 * (x // 2)].reshape(16, 128)
             if x % 2:
                 late = pltpu.roll(late, LOCAL, 1)
-            block = jnp.concatenate([total[:, 8 * x : 8 * x + 8], late.reshape(4, 8, 128)], axis=1)
-            block_send[4 * h : 4 * h + 4, x] = block.astype(BF16)
-        for a in range(4):
-            hop = (4 * h + a + 2) % 8
+            block = jnp.concatenate([total[:, 8 * x : 8 * x + 8], late.reshape(2, 8, 128)], axis=1)
+            block_send[2 * q : 2 * q + 2, x] = block.astype(BF16)
+        for a in range(2):
+            spot = 2 * q + a
+            hop = (spot + 3) % 8
             for i in ((2, 1, 3) if hop == 0 else (2, 1, 3, 0)):
                 x = lax.rem(ex + i, 4)
                 other = lax.rem(zed + hop, 8) * 4 + x
                 copy = pltpu.make_async_remote_copy(
-                    src_ref=block_send.at[4 * h + a, x], dst_ref=block_recv.at[ch],
-                    send_sem=q_send.at[4 * (4 * h + a) + i], recv_sem=q_recv.at[ch],
+                    src_ref=block_send.at[spot, x], dst_ref=block_recv.at[ch],
+                    send_sem=q_send.at[4 * spot + i], recv_sem=q_recv.at[ch],
                     device_id={"chan": other}, device_id_type=MESH,
                 )
                 copy.start()
                 chan_copies.append(copy)
 
-    block_recv[ch] = block_send[6, ex]
-    lhs[0:32, :] = jnp.zeros((32, 512), F32)
-    lhs[128:160, :] = jnp.zeros((32, 512), F32)
+    block_recv[ch] = block_send[5, ex]
 
     @pl.loop(1, CHANS)
     def _(i):
@@ -345,7 +346,7 @@
     for group in (halves_up, halves_down, direct_up, direct_down, passed_up, passed_down):
         for copy in group:
             copy.wait_send()
-    for copy in base_copies + part_copies[0] + part_copies[1]:
+    for copy in base_copies + sum(part_copies.values(), []):
         copy.wait_send()
     for copy in chan_copies:
         copy.wait_send()
@@ -354,14 +355,16 @@
 
 
 def search(voltages, positions, chan_delays, sub_delays):
-    vmem, anywhere = pl.BlockSpec(memory_space=pltpu.VMEM), pl.BlockSpec(memory_space=pl.ANY)
+    hbm = pl.BlockSpec(memory_space=pltpu.HBM)
     dma = pltpu.SemaphoreType.DMA
     return pl.pallas_call(
         kernel,
-        out_shape=jax.ShapeDtypeStruct((8 * SPAN_V, ND), F32),
-        in_specs=[anywhere, vmem, anywhere, vmem],
-        out_specs=vmem,
+        out_shape=pltpu.VMEM((8 * SPAN_V, ND), F32),
+        in_specs=[hbm, hbm, hbm, hbm],
+        out_specs=pl.BlockSpec(memory_space=pltpu.VMEM),
         scratch_shapes=[
+            pltpu.VMEM((8, 128), jnp.int32),
+            pltpu.VMEM((CHANS, ND), jnp.int32),
             pltpu.VMEM((2, SPAN, 256, 256), BF16),
             pltpu.VMEM((4, CHUNKS, 512, 256), BF16),
             pltpu.VMEM((CHUNKS, 3, 512, 256), BF16),
@@ -377,8 +380,9 @@
             pltpu.VMEM((SUBCH, 256), F32),
             pltpu.VMEM(((SPAN + D1MAX) * LOCAL, 256), BF16),
             pltpu.VMEM((D2MAX + 1, 512, ND), BF16),
-            pltpu.VMEM((2, 3, 4, 48, 128), BF16),
-            pltpu.VMEM((2, 3, 4, 48, 128), BF16),
+            pltpu.VMEM((4, 4, 2, 48, 128), F32),
+            pltpu.VMEM((4, 4, 2, 48, 128), BF16),
+            pltpu.VMEM((4, 3, 2, 48, 128), BF16),
             pltpu.VMEM((8, 4, 16, 128), BF16),
             pltpu.VMEM((CHANS, 16, 128), BF16),
             pltpu.VMEM((160, 512), F32),
@@ -387,14 +391,16 @@
             pltpu.VMEM((4, 32, 256), F32),
             dma((CHUNKS,)),
             dma,
+            dma,
+            dma,
             dma((6 * CHUNKS,)),
             dma((6 * CHUNKS,)),
             dma,
             dma,
             dma((2,)),
             dma((2,)),
-            dma((6,)),
-            dma((6,)),
+            dma((12,)),
+            dma((12,)),
             dma((CHANS,)),
             dma((CHANS,)),
             dma,
@@ -412,7 +418,8 @@
     )
 
 
-def boxcar_kernel(box_ref, ext_ref, out_ref):
+def boxcar_kernel(box_ref, ext_ref, out_ref, held, sems):
+    copies = []
     for filter_index in range(NW):
         width_now = box_ref[0, filter_index]
         stride_now = box_ref[1, filter_index]
@@ -422,16 +429,23 @@
             start = jnp.minimum(offset * stride_now, BOXMAX)
             kept = jnp.where(offset < width_now, 1.0, 0.0)
             summed = summed + ext_ref[pl.ds(start, SPAN)] * kept
-        out_ref[:, filter_index] = summed * gain[None]
+        held[filter_index] = summed * gain[None]
+        copies.append(
+            pltpu.make_async_copy(held.at[filter_index], out_ref.at[:, filter_index], sems.at[filter_index])
+        )
+        copies[-1].start()
+    for copy in copies:
+        copy.wait()
 
 
 def boxcar_filter(extended, boxcars):
-    vmem = pl.BlockSpec(memory_space=pltpu.VMEM)
     filtered = pl.pallas_call(
         boxcar_kernel,
         out_shape=jax.ShapeDtypeStruct((SPAN, NW, 8, ND), F32),
-        in_specs=[pl.BlockSpec(memory_space=pltpu.SMEM), vmem],
-        out_specs=vmem,
+        in_specs=[pl.BlockSpec(memory_space=pltpu.SMEM), pl.BlockSpec(memory_space=pltpu.VMEM)],
+        out_specs=pl.BlockSpec(memory_space=pl.ANY),
+        scratch_shapes=[pltpu.VMEM((NW, SPAN, 8, ND), F32), pltpu.SemaphoreType.DMA((NW,))],
+        compiler_params=pltpu.CompilerParams(vmem_limit_bytes=8 * 1024 * 1024),
         name="boxcar",
     )(jnp.transpose(boxcars), extended)
     return jnp.transpose(filtered, (2, 0, 1, 3))

time: 66.8 us -> 64.7 us (0.969)
  Pallas kernels: 66.6 us -> 64.6 us
    pallas_call x1, Pallas kernels: 64.9 us -> 63.3 us  [search(): pl.pallas_call(kernel, out_shape=pltpu.VMEM((8 * SPAN_V, ND), F32), in_sp...]
where the time goes in v4:
time: 64.7 us; the launch traced here: 64.6 us
  Pallas kernels  64.6 us (100%)
    pallas_call x1, Pallas kernels, search(): pl.pallas_call(kernel, out_shape=pltpu.VMEM((8 * SPAN_V, ND), F32), in_sp...  63.3 us
    pallas_call x1, Pallas kernels, boxcar_filter(): pl.pallas_call(boxcar_kernel, out_shape=jax.ShapeDtypeStruct((SPAN, NW, 8...  1.32 us

profile of v4, /device:TPU:1, one launch (start us, length us, event | category | flops | bytes accessed | tf_op | source)
XLA Modules:
  0.0 64.6 jit_solution(5777800996463392501)
XLA Ops:
  0.0 0.0 copy-start
  0.0 63.3 %search.1 = f32[144,256]{1,0:T(8,128)S(1)} custom-call(bf16[2,12,256,256]{3,2,1,0:T(8,128)(2,1)} %bitcast.8, s32[8,128]{1,0:T(8,128)} %bitcast.10, s32[16,8192]{1,0:T(8,128)} %cd_ref.1, s32[32,256]{1,0:T(8,128)} %bitcast.9), custom_call_target="tpu_custom_call" | custom-call | tf_op jit(solution)/shard_map/search/pallas_call | solution.py:360
  63.3 0.0 copy-done
  63.3 1.3 %boxcar.1 = f32[12,3,8,256]{3,2,1,0:T(8,128)} custom-call(s32[2,3]{1,0:T(2,128)S(1)} %bitcast.7, f32[18,8,256]{2,1,0:T(8,128)S(1)} %bitcast.6), custom_call_target="tpu_custom_call" | custom-call | tf_op jit(solution)/shard_map/boxcar/pallas_call | solution.py:442
Async XLA Ops:
  0.0 63.3 %copy-start = (s32[3,2]{0,1:T(2,128)S(1)}, s32[3,2]{0,1:T(2,128)}, u32[]{:S(2)}) copy-start(s32[3,2]{0,1:T(2,128)} %param.9) | copy-start | bytes 76

commit v5 on v4

--- a/solution.py
+++ b/solution.py
@@ -43,7 +43,7 @@
     pos_ref, sd_ref, vbuf, packed, arrived, relay_up, relay_down, table, acc, power,
     rim, base_own, base_other, cdbuf, delay_t, chooser, weights,
     part_own, part_send, part_recv, block_send, block_recv, lhs, swap_send, swap_recv, trig,
-    v_sem, cd_sem, pos_sem, sd_sem, a_send, a_recv, r_send, r_recv, b_send, b_recv, p_send, p_recv, q_send, q_recv, s_send, s_recv,
+    v_sem, cd_sem, pos_sem, sd_sem, a_send, a_recv, r_send, r_recv, b_send, b_recv, p_send, p_recv, q_send, q_recv, s_send, s_recv, word,
 ):
     sec = lax.axis_index("section")
     ch = lax.axis_index("chan")
@@ -52,15 +52,13 @@
     up, down, far = lax.rem(fd + 1, 4), lax.rem(fd + 3, 4), lax.rem(fd + 2, 4)
 
     barrier = pltpu.get_barrier_semaphore()
-    for other in (up, down, far):
+    beside = [lax.rem(zed + n, 8) * 4 + ex for n in (1, 7)]
+    across = [zed * 4 + lax.rem(ex + n, 4) for n in (1, 3)]
+    pl.semaphore_signal(barrier, inc=1, device_id={"section": 1 - sec}, device_id_type=MESH)
+    for other in (far, up, down):
         pl.semaphore_signal(barrier, inc=1, device_id={"feed": other}, device_id_type=MESH)
-    pl.semaphore_signal(barrier, inc=1, device_id={"section": 1 - sec}, device_id_type=MESH)
-
-    @pl.loop(1, CHANS)
-    def _(i):
-        pl.semaphore_signal(
-            barrier, inc=1, device_id={"chan": lax.rem(ch + i, CHANS)}, device_id_type=MESH
-        )
+    for other in beside + across:
+        pl.semaphore_signal(barrier, inc=1, device_id={"chan": other}, device_id_type=MESH)
 
     loads = []
     for j in range(CHUNKS):
@@ -91,7 +89,7 @@
                     packed[2 * tile, j, rows, pl.ds(128 * pair, 128)] = even
                     packed[2 * tile + 1, j, rows, pl.ds(128 * pair, 128)] = odd
 
-    pl.semaphore_wait(barrier, 3 + 1 + CHANS - 1)
+    pl.semaphore_wait(barrier, 8)
 
     def to_feed(src, dst, sems, index, other):
         copy = pltpu.make_async_remote_copy(
@@ -110,6 +108,14 @@
     for j in range(CHUNKS):
         direct_up.append(to_feed(packed.at[up, j], arrived.at[j, 0], a_sems, 6 * j + 2, up))
         direct_down.append(to_feed(packed.at[down, j], arrived.at[j, 1], a_sems, 6 * j + 3, down))
+
+    def tell(n, others):
+        if n:
+            pl.semaphore_wait(word.at[n - 1], 2)
+        for other in others:
+            pl.semaphore_signal(word.at[n], inc=1, device_id={"chan": other}, device_id_type=MESH)
+
+    tell(0, across)
 
     step = 2.0 * math.pi / NF
     pos_load.wait()
@@ -158,11 +164,14 @@
             rows = pl.ds(pl.multiple_of(512 * m, 512), 512)
             acc[j, rows, :] = block_dot(0, rows, packed[fd, j])
 
+    tell(1, beside)
     for j in range(CHUNKS):
         halves_up[j].wait_recv()
         passed_up.append(to_feed(relay_up.at[j], arrived.at[j, 2, re_rows], a_sems, 6 * j + 4, up))
         halves_down[j].wait_recv()
         passed_down.append(to_feed(relay_down.at[j], arrived.at[j, 2, im_rows], a_sems, 6 * j + 5, down))
+
+    tell(2, beside)
 
     cd_load.wait()
     one_k = (row_ids((NK, 256)) == (lane_ids((NK, 256)) & (NK - 1))).astype(BF16)
@@ -190,6 +199,7 @@
         for d in range(D2MAX + 1):
             weights[d, rows, :] = jnp.where(own_k & (delay == d), 1.0, 0.0).astype(BF16)
 
+    tell(3, beside)
     for j in range(CHUNKS):
         direct_up[j].wait_recv()
         direct_down[j].wait_recv()
@@ -198,6 +208,9 @@
         def _(m):
             rows = pl.ds(pl.multiple_of(512 * m, 512), 512)
             acc[j, rows, :] += block_dot(1, rows, arrived[j, 0]) + block_dot(2, rows, arrived[j, 1])
+
+    tell(4, beside)
+    pl.semaphore_wait(word.at[4], 2)
 
     def beam_power(j, m):
         rows = pl.ds(pl.multiple_of(512 * m, 512), 512)
@@ -405,6 +418,7 @@
             dma((CHANS,)),
             dma,
             dma,
+            pltpu.SemaphoreType.REGULAR((5,)),
         ],
         compiler_params=pltpu.CompilerParams(
             collective_id=0, has_side_effects=True, vmem_limit_bytes=60 * 1024 * 1024

time: 64.7 us -> 63.3 us (0.978)
  Pallas kernels: 64.6 us -> 63.2 us
    pallas_call x1, Pallas kernels: 63.3 us -> 61.9 us  [search(): pl.pallas_call(kernel, out_shape=pltpu.VMEM((8 * SPAN_V, ND), F32), in_sp...]
where the time goes in v5:
time: 63.3 us; the launch traced here: 63.2 us
  Pallas kernels  63.2 us (100%)
    pallas_call x1, Pallas kernels, search(): pl.pallas_call(kernel, out_shape=pltpu.VMEM((8 * SPAN_V, ND), F32), in_sp...  61.9 us
    pallas_call x1, Pallas kernels, boxcar_filter(): pl.pallas_call(boxcar_kernel, out_shape=jax.ShapeDtypeStruct((SPAN, NW, 8...  1.32 us

profile of v5, /device:TPU:1, one launch (start us, length us, event | category | flops | bytes accessed | tf_op | source)
XLA Modules:
  0.0 63.2 jit_solution(15352948883789921620)
XLA Ops:
  0.0 0.0 copy-start
  0.0 61.9 %search.1 = f32[144,256]{1,0:T(8,128)S(1)} custom-call(bf16[2,12,256,256]{3,2,1,0:T(8,128)(2,1)} %bitcast.8, s32[8,128]{1,0:T(8,128)} %bitcast.10, s32[16,8192]{1,0:T(8,128)} %cd_ref.1, s32[32,256]{1,0:T(8,128)} %bitcast.9), custom_call_target="tpu_custom_call" | custom-call | tf_op jit(solution)/shard_map/search/pallas_call | solution.py:373
  61.9 0.0 copy-done
  61.9 1.3 %boxcar.1 = f32[12,3,8,256]{3,2,1,0:T(8,128)} custom-call(s32[2,3]{1,0:T(2,128)S(1)} %bitcast.7, f32[18,8,256]{2,1,0:T(8,128)S(1)} %bitcast.6), custom_call_target="tpu_custom_call" | custom-call | tf_op jit(solution)/shard_map/boxcar/pallas_call | solution.py:456
Async XLA Ops:
  0.0 61.9 %copy-start = (s32[3,2]{0,1:T(2,128)S(1)}, s32[3,2]{0,1:T(2,128)}, u32[]{:S(2)}) copy-start(s32[3,2]{0,1:T(2,128)} %param.9) | copy-start | bytes 76

commit v6 on v5

--- a/solution.py
+++ b/solution.py
@@ -74,6 +74,17 @@
     sd_load = pltpu.make_async_copy(sd_any, sd_ref, sd_sem)
     sd_load.start()
 
+    def to_feed(src, dst, sems, index, other):
+        copy = pltpu.make_async_remote_copy(
+            src_ref=src, dst_ref=dst, send_sem=sems[0].at[index], recv_sem=sems[1].at[index],
+            device_id={"feed": other}, device_id_type=MESH,
+        )
+        copy.start()
+        return copy
+
+    a_sems = (a_send, a_recv)
+    halves_up, halves_down, direct_up, direct_down, passed_up, passed_down = [], [], [], [], [], []
+    re_rows, im_rows = pl.ds(0, 256), pl.ds(256, 256)
     low_half = lane_ids((256, 128)) < LOCAL
     for j in range(CHUNKS):
         loads[j].wait()
@@ -88,21 +99,8 @@
                     rows = pl.ds(256 * part, 256)
                     packed[2 * tile, j, rows, pl.ds(128 * pair, 128)] = even
                     packed[2 * tile + 1, j, rows, pl.ds(128 * pair, 128)] = odd
-
-    pl.semaphore_wait(barrier, 8)
-
-    def to_feed(src, dst, sems, index, other):
-        copy = pltpu.make_async_remote_copy(
-            src_ref=src, dst_ref=dst, send_sem=sems[0].at[index], recv_sem=sems[1].at[index],
-            device_id={"feed": other}, device_id_type=MESH,
-        )
-        copy.start()
-        return copy
-
-    a_sems = (a_send, a_recv)
-    halves_up, halves_down, direct_up, direct_down, passed_up, passed_down = [], [], [], [], [], []
-    re_rows, im_rows = pl.ds(0, 256), pl.ds(256, 256)
-    for j in range(CHUNKS):
+        if j == 0:
+            pl.semaphore_wait(barrier, 8)
         halves_up.append(to_feed(packed.at[far, j, re_rows], relay_up.at[j], a_sems, 6 * j, up))
         halves_down.append(to_feed(packed.at[far, j, im_rows], relay_down.at[j], a_sems, 6 * j + 1, down))
     for j in range(CHUNKS):

time: 63.3 us -> 63.4 us (level)
  no operation moved by 1% of the time
where the time goes in v6:
time: 63.4 us
  Pallas kernels  63.3 us (100%)
    pallas_call x1, Pallas kernels, search(): pl.pallas_call(kernel, out_shape=pltpu.VMEM((8 * SPAN_V, ND), F32), in_sp...  62 us
    pallas_call x1, Pallas kernels, boxcar_filter(): pl.pallas_call(boxcar_kernel, out_shape=jax.ShapeDtypeStruct((SPAN, NW, 8...  1.32 us

profile of v6, /device:TPU:1, one launch (start us, length us, event | category | flops | bytes accessed | tf_op | source)
XLA Modules:
  0.0 63.4 jit_solution(12259878378457081851)
XLA Ops:
  0.0 0.0 copy-start
  0.0 62.0 %search.1 = f32[144,256]{1,0:T(8,128)S(1)} custom-call(bf16[2,12,256,256]{3,2,1,0:T(8,128)(2,1)} %bitcast.8, s32[8,128]{1,0:T(8,128)} %bitcast.10, s32[16,8192]{1,0:T(8,128)} %cd_ref.1, s32[32,256]{1,0:T(8,128)} %bitcast.9), custom_call_target="tpu_custom_call" | custom-call | tf_op jit(solution)/shard_map/search/pallas_call | solution.py:371
  62.0 0.0 copy-done
  62.0 1.3 %boxcar.1 = f32[12,3,8,256]{3,2,1,0:T(8,128)} custom-call(s32[2,3]{1,0:T(2,128)S(1)} %bitcast.7, f32[18,8,256]{2,1,0:T(8,128)S(1)} %bitcast.6), custom_call_target="tpu_custom_call" | custom-call | tf_op jit(solution)/shard_map/boxcar/pallas_call | solution.py:454
Async XLA Ops:
  0.0 62.0 %copy-start = (s32[3,2]{0,1:T(2,128)S(1)}, s32[3,2]{0,1:T(2,128)}, u32[]{:S(2)}) copy-start(s32[3,2]{0,1:T(2,128)} %param.9) | copy-start | bytes 76
